TPU v7x, 512 devices: a whole 4x4x16 slice. The times are simulated.
512 devices in a mesh: prow: 16 (over x, y), pcol: 32 (over z, core).
Axes of the slice: x: 4, y: 4, z: 16, core: 2. Of those that a mesh axis runs over, the one named last changes fastest.
Arguments:
- adjoint_trail: float32 [2, 16, 256, 1, 32, 256], P(None, 'prow', None, None, 'pcol'), as said below
- factor_low: float32 [2, 16, 32, 8, 4, 256], P(None, 'prow', 'pcol'), may hold values from -0.0625 to 0.0625
- adjoint_low: float32 [2, 16, 32, 8, 4, 256], P(None, 'prow', 'pcol'), may hold values from -6 to 6
- factor_top: float32 [10, 256, 256], P(None, 'pcol'), as said below
- adjoint_top: float32 [10, 256, 256], P(None, 'pcol'), may hold values from -6 to 6
- diag_inverse: float32 [4, 256, 256], P(None, 'pcol'), as said below
Outputs:
- grad_low: float32 [2, 16, 32, 8, 4, 256], P(None, 'prow', 'pcol')
- grad_top: float32 [10, 256, 256], P(None, 'pcol')
Inputs may be any that keep to these rules, and one draw needn't show every extreme that they name: adjoint_trail reshaped row-major to 8192 x 8192 is symmetric. The diagonal blocks factor_top[j (j + 1) / 2 + j] are lower triangular with a positive diagonal. diag_inverse[j] is the inverse of factor_top[j (j + 1) / 2 + j].
All inputs are finite; a program needn't handle non-finite values.
Results may differ from a plain program's by a relative error of at most 0.00024.
Values sent between devices are 32-bit elements; how exact they have to be, the bound alone decides.
A program may use at most 64 MiB of HBM per device.

v0:
```python
import jax
import jax.numpy as jnp
from jax import lax
from jax.sharding import PartitionSpec as P

NB = 256
K = 4
HIGHEST = lax.Precision.HIGHEST


def from_root(array, axis, root):
    mine = lax.axis_index(axis) == root
    return lax.psum(jnp.where(mine, array, jnp.zeros_like(array)), axis)


def matmul(left, right):
    return jnp.dot(left, right, precision=HIGHEST, preferred_element_type=jnp.float32)


def inner_product(left, right):
    return lax.dot_general(
        left, right, (((0,), (0,)), ((), ())), precision=HIGHEST, preferred_element_type=jnp.float32
    )


def block_slot(row_block, col_block):
    return row_block * (row_block + 1) // 2 + col_block


def half_lower(square):
    size = square.shape[0]
    row_ids = lax.broadcasted_iota(jnp.int32, (size, size), 0)
    col_ids = lax.broadcasted_iota(jnp.int32, (size, size), 1)
    return jnp.where(row_ids > col_ids, square, jnp.where(row_ids == col_ids, 0.5 * square, 0.0))


def diagonal_adjoint(diagonal, inverse, lower_adj):
    inner = half_lower(inner_product(jnp.tril(diagonal), lower_adj))
    spread = inner_product(inverse, matmul(inner, inverse))
    return 0.5 * (spread + spread.T)


def rows_one(piece):
    return lax.all_gather(piece, "pcol", axis=1, tiled=True)


def owner_one(piece, root):
    return from_root(piece, "prow", root)


def reduce_one(term, count):
    return lax.psum_scatter(
        term(jnp.int32(0), lax.axis_size("pcol") * count), "pcol", scatter_dimension=0, tiled=True
    )


def trailing_product(trail, panels, gather_rows, send_owner, reduce_rows):
    prow_count = lax.axis_size("prow")
    pcol_count = lax.axis_size("pcol")
    cycles, sub_rows, width = panels.shape
    block = sub_rows * pcol_count
    gathered = gather_rows(panels[:, None]).reshape(cycles, block, width)
    column = lax.axis_index("pcol")
    col_cycles = trail.shape[3]
    global_block = 0 + column
    share = lax.dynamic_index_in_dim(gathered, global_block // prow_count, 0, keepdims=False)
    owned = [send_owner(share, global_block % prow_count)]
    stacked = jnp.stack(owned)
    view = trail.reshape(cycles, pcol_count, sub_rows, col_cycles, block)
    unit = cycles * sub_rows

    def term(start, count):
        product = jnp.einsum(
            "iaekb,kbn->aien", view, stacked, precision=HIGHEST, preferred_element_type=jnp.float32
        )
        return product.reshape(count, width)

    return reduce_rows(term, unit).reshape(cycles, sub_rows, width)


def per_device(adjoint_trail, factor_low, adjoint_low, factor_top, adjoint_top, diag_inverse):
    cycles = factor_low.shape[0]
    sub_rows = factor_low.shape[3]
    local_rows = cycles * sub_rows
    low_factor = factor_low.reshape(cycles, sub_rows, K * NB)
    low_adjoint = adjoint_low.reshape(local_rows, K, NB)
    columns = low_factor.reshape(local_rows, K, NB)
    top_factor, top_adjoint, inverses = (
        lax.all_gather(factor_top, "pcol", axis=1, tiled=True),
        lax.all_gather(adjoint_top, "pcol", axis=1, tiled=True),
        lax.all_gather(diag_inverse, "pcol", axis=1, tiled=True),
    )
    lower_grads = [None] * K
    diag_grads = [None] * K
    upper_grads = {}
    grams = {}

    def lower_step(panel):
        single = low_factor[:, :, panel * NB : (panel + 1) * NB]
        image = trailing_product(adjoint_trail, single, rows_one, owner_one, reduce_one).reshape(
            local_rows, NB
        )
        residual = low_adjoint[:, panel] - 2.0 * image
        for later in range(panel + 1, K):
            residual = residual - matmul(lower_grads[later], top_factor[block_slot(later, panel)])
        lower_grads[panel] = matmul(residual, inverses[panel])

    def top_step(panel):
        for row_block in range(panel + 1, K):
            top_residual = top_adjoint[block_slot(row_block, panel)] - grams[row_block, panel]
            top_residual = top_residual - 2.0 * matmul(
                diag_grads[row_block], top_factor[block_slot(row_block, panel)]
            )
            for middle in range(panel + 1, row_block):
                top_residual = top_residual - matmul(
                    upper_grads[middle, row_block], top_factor[block_slot(middle, panel)]
                )
            for beyond in range(row_block + 1, K):
                top_residual = top_residual - inner_product(
                    upper_grads[row_block, beyond], top_factor[block_slot(beyond, panel)]
                )
            upper_grads[panel, row_block] = matmul(top_residual, inverses[panel])
        lower_adj = top_adjoint[block_slot(panel, panel)] - grams[panel, panel]
        for row_block in range(panel + 1, K):
            lower_adj = lower_adj - inner_product(
                upper_grads[panel, row_block], top_factor[block_slot(row_block, panel)]
            )
        diag_grads[panel] = diagonal_adjoint(
            top_factor[block_slot(panel, panel)], inverses[panel], jnp.tril(lower_adj)
        )

    for panel in reversed(range(K)):
        lower_step(panel)
        local_gram = jnp.stack(
            [inner_product(lower_grads[panel], columns[:, earlier]) for earlier in range(panel + 1)]
        )
        summed = lax.psum(local_gram, ("prow", "pcol"))
        for earlier in range(panel + 1):
            grams[panel, earlier] = summed[earlier]
        top_step(panel)
    grad_low = jnp.stack(lower_grads, 1).reshape(factor_low.shape)
    blocks = []
    for row_block in range(K):
        for col_block in range(row_block + 1):
            if row_block == col_block:
                blocks.append(diag_grads[col_block])
            else:
                blocks.append(upper_grads[col_block, row_block])
    full_top = jnp.stack(blocks)
    share_rows = factor_top.shape[1]
    grad_top = lax.dynamic_slice_in_dim(
        full_top, lax.axis_index("pcol") * share_rows, share_rows, 1
    )
    return (grad_low, grad_top)


def solution(mesh):
    in_specs = (
        P(None, "prow", None, None, "pcol", None),
        P(None, "prow", "pcol", None, None, None),
        P(None, "prow", "pcol", None, None, None),
        P(None, "pcol", None),
        P(None, "pcol", None),
        P(None, "pcol", None),
    )
    out_specs = (P(None, "prow", "pcol", None, None, None), P(None, "pcol", None))
    return jax.shard_map(
        per_device, mesh=mesh, in_specs=in_specs, out_specs=out_specs, check_vma=False
    )
```

profile of v0, /device:TPU:8, one launch (start us, length us, event | category | flops | bytes accessed | tf_op | source)
XLA Modules:
  0.0 1294.8 jit_solution(6312719842912323253)
XLA Ops:
  9.0 37.8 %all-gather.3 = f32[2,256,256]{2,1,0:T(8,128)S(1)} all-gather(f32[2,8,256]{2,1,0:T(8,128)S(1)} %get-tuple-element.15), channel_id=5, replica_groups=mesh['prow'=16,'pcol'=32] {'pcol'}, dimensions={1}, use_global_device_ids=true | all-gather | bytes 540672 | tf_op jit(solution)/shard_map/all_gather | solution.py:44
  46.8 28.5 %all-gather.2 = f32[2,256,256]{2,1,0:T(8,128)S(1)} all-gather(f32[2,8,256]{2,1,0:T(8,128)S(1)} %get-tuple-element.16), channel_id=4, replica_groups=mesh['prow'=16,'pcol'=32] {'pcol'}, dimensions={1}, use_global_device_ids=true | all-gather | bytes 540672 | tf_op jit(solution)/shard_map/all_gather | solution.py:44
  76.7 29.8 %all-gather.1 = f32[2,256,256]{2,1,0:T(8,128)S(1)} all-gather(f32[2,8,256]{2,1,0:T(8,128)S(1)} %get-tuple-element.17), channel_id=3, replica_groups=mesh['prow'=16,'pcol'=32] {'pcol'}, dimensions={1}, use_global_device_ids=true | all-gather | bytes 540672 | tf_op jit(solution)/shard_map/all_gather | solution.py:44
  107.3 28.5 %all-gather = f32[2,256,256]{2,1,0:T(8,128)S(1)} all-gather(f32[2,8,256]{2,1,0:T(8,128)S(1)} %get-tuple-element.14), channel_id=2, replica_groups=mesh['prow'=16,'pcol'=32] {'pcol'}, dimensions={1}, use_global_device_ids=true | all-gather | bytes 540672 | tf_op jit(solution)/shard_map/all_gather | solution.py:44
  137.2 113.6 %all-reduce.7.cloned.1.call-done = (f32[256,256]{1,0:T(8,128)}, f32[256,256]{1,0:T(8,128)}, f32[256,256]{1,0:T(8,128)}, f32[256,256]{1,0:T(8,128)}) async-done(((f32[256,256]{1,0:T(8,128)}, f32[256,256]{1,0:T(8,128)}, f32[256,256]{1,0:T(8,128)}, f32[256,256]{1,0:T(8,128)}), (f32[256,256]{1,0:T(8,128)}, f32[256,256]{1,0:T(8,128)}, f32[256,256]{1,0:T(8,128)}, ...) | async-done | bytes 1048592 | tf_op jit(solution)/shard_map/psum | solution.py:13
  250.9 1.7 convolution_bitcast_fusion
  252.5 1.1 copy.31
  254.4 1.2 copy.29
  257.0 1.1 copy.27
  258.9 1.1 copy.25
  261.1 99.8 %reduce-scatter.11.cloned.1.call-done = f32[16,256]{1,0:T(8,128)} async-done(((f32[512,256]{1,0:T(8,128)}), f32[16,256]{1,0:T(8,128)}) %reduce-scatter.11.cloned.1.call-update) | async-done | bytes 16400 | tf_op jit(solution)/shard_map/reduce_scatter | solution.py:52
  360.9 1.2 fusion.67
  363.8 1.0 pad_maximum_fusion
  364.8 104.2 %reduce-scatter.9.cloned.1.call-done = f32[16,256]{1,0:T(8,128)} async-done(((f32[512,256]{1,0:T(8,128)}), f32[16,256]{1,0:T(8,128)}) %reduce-scatter.9.cloned.1.call-update) | async-done | bytes 16400 | tf_op jit(solution)/shard_map/reduce_scatter | solution.py:52
  469.0 72.4 %all-gather.10.cloned.1.call-done = f32[10,256,256]{2,1,0:T(8,128)} async-done(((f32[10,8,256]{2,1,0:T(8,128)}), f32[10,256,256]{2,1,0:T(8,128)}) %all-gather.10.cloned.1.call-update) | async-done | bytes 2621456 | tf_op jit(solution)/shard_map/all_gather | solution.py:89
  541.4 1.3 convolution_subtract_fusion.19
  542.8 1.1 fusion.70
  545.2 103.2 %reduce-scatter.7.cloned.1.call-done = f32[16,256]{1,0:T(8,128)} async-done(((f32[512,256]{1,0:T(8,128)}), f32[16,256]{1,0:T(8,128)}) %reduce-scatter.7.cloned.1.call-update) | async-done | bytes 16400 | tf_op jit(solution)/shard_map/reduce_scatter | solution.py:52
  648.4 1.2 convolution_subtract_fusion.18
  649.6 1.2 convolution_subtract_fusion.17
  650.8 1.1 fusion.74
  652.0 1.1 convolution_bitcast_fusion.11
  653.1 1.1 convolution_bitcast_fusion.12
  654.2 102.5 %reduce-scatter.5.cloned.1.call-done = f32[16,256]{1,0:T(8,128)} async-done(((f32[512,256]{1,0:T(8,128)}), f32[16,256]{1,0:T(8,128)}) %reduce-scatter.5.cloned.1.call-update) | async-done | bytes 16400 | tf_op jit(solution)/shard_map/reduce_scatter | solution.py:52
  758.2 1.2 fusion.79
  759.4 1.2 convolution_bitcast_fusion.13
  760.5 1.9 pad_maximum_fusion.2
  762.4 1.0 pad_maximum_fusion.1
  764.3 65.2 %all-gather.12.cloned.1.call-done = f32[10,256,256]{2,1,0:T(8,128)} async-done(((f32[10,8,256]{2,1,0:T(8,128)}), f32[10,256,256]{2,1,0:T(8,128)}) %all-gather.12.cloned.1.call-update) | async-done | bytes 2621456 | tf_op jit(solution)/shard_map/all_gather | solution.py:90
  829.5 417.1 %all-reduce.5.cloned.1.call-done = (f32[2,256,256]{2,1,0:T(8,128)}, f32[3,256,256]{2,1,0:T(8,128)}, f32[4,256,256]{2,1,0:T(8,128)}, f32[1,256,256]{2,1,0:T(8,128)}) async-done(((f32[2,256,256]{2,1,0:T(8,128)}, f32[3,256,256]{2,1,0:T(8,128)}, f32[4,256,256]{2,1,0:T(8,128)}, f32[1,256,256]{2,1,0:T(8,128)}), (f32[2,256,256]{2,1,0:T(8,128)}, f32[3,256,256]{2,1,0:T(8,128)}, f32[4,256,256]{2,1,0:T(8,128)}, ...) | async-done | bytes 2621456 | tf_op jit(solution)/shard_map/psum | solution.py:137
  1246.6 1.5 fusion.18
  1248.1 1.3 fusion.62
  1249.5 1.5 fusion.66
  1251.2 1.5 fusion.8
  1252.7 1.3 fusion.69
  1254.0 1.6 fusion.7
  1258.0 1.5 fusion.5
  1260.0 1.3 fusion.72
  1261.3 1.5 fusion.6
  1264.8 1.6 convolution_subtract_fusion.11
  1267.9 1.3 fusion.71
  1269.2 1.8 copy.38
  1271.0 1.5 fusion.1
  1272.5 1.5 fusion.2
  1276.7 1.4 fusion.3
  1279.8 1.6 convolution_subtract_fusion.6
  1284.4 1.0 bitcast_dynamic-update-slice_fusion.8
  1285.4 1.1 bitcast_dynamic-update-slice_fusion.7
  (138 shorter events, 27.5 us)
Async XLA Ops:
  8.0 242.9 %all-reduce.7.cloned.1.call-start = ((), (), s32[]{:S(2)}) async-start(), calls=%async_computation.12 | async-start | bytes 2097152 | tf_op jit(solution)/shard_map/psum | solution.py:13
  9.0 128.2 %copy-start.19 = (f32[2,1,256,1,1,256]{5,4,3,2,1,0:T(1,128)S(1)}, f32[2,1,256,1,1,256]{5,4,3,2,1,0:T(1,128)}, u32[]{:S(2)}) copy-start(f32[2,1,256,1,1,256]{5,4,3,2,1,0:T(1,128)} %param.6) | copy-start | bytes 1572868
  136.6 124.5 %all-gather.8.cloned.1.call-start = ((), (), s32[]{:S(2)}) async-start(), calls=%async_computation.8 | async-start | bytes 1081344 | tf_op jit(solution)/shard_map/all_gather | solution.py:91
  137.1 223.8 %reduce-scatter.11.cloned.1.call-start = ((), (), s32[]{:S(2)}) async-start(), calls=%async_computation.7 | async-start | bytes 540672 | tf_op jit(solution)/shard_map/reduce_scatter | solution.py:52
  250.8 2.9 copy-start.25
  250.9 5.5 copy-start.24
  253.7 215.4 %reduce-scatter.9.cloned.1.call-start = ((), (), s32[]{:S(2)}) async-start(), calls=%async_computation.6 | async-start | bytes 540672 | tf_op jit(solution)/shard_map/reduce_scatter | solution.py:52
  253.7 4.6 copy-start.23
  255.6 285.9 %all-gather.10.cloned.1.call-start = ((), (), s32[]{:S(2)}) async-start(), calls=%async_computation.9 | async-start | bytes 2703360 | tf_op jit(solution)/shard_map/all_gather | solution.py:89
  256.3 392.1 %reduce-scatter.7.cloned.1.call-start = ((), (), s32[]{:S(2)}) async-start(), calls=%async_computation.5 | async-start | bytes 540672 | tf_op jit(solution)/shard_map/reduce_scatter | solution.py:52
  256.4 4.6 copy-start.27
  257.0 3.9 copy-start.26
  258.2 498.6 %reduce-scatter.5.cloned.1.call-start = ((), (), s32[]{:S(2)}) async-start(), calls=%async_computation.4 | async-start | bytes 540672 | tf_op jit(solution)/shard_map/reduce_scatter | solution.py:52
  260.1 569.4 %all-gather.12.cloned.1.call-start = ((), (), s32[]{:S(2)}) async-start(), calls=%async_computation.10 | async-start | bytes 2703360 | tf_op jit(solution)/shard_map/all_gather | solution.py:90
  260.7 985.9 %all-reduce.5.cloned.1.call-start = ((), (), s32[]{:S(2)}) async-start(), calls=%async_computation.11 | async-start | bytes 5242880 | tf_op jit(solution)/shard_map/psum | solution.py:137
  541.4 215.3 %copy-start = (f32[10,256,256]{2,1,0:T(8,128)S(1)}, f32[10,256,256]{2,1,0:T(8,128)}, u32[]{:S(2)}) copy-start(f32[10,256,256]{2,1,0:T(8,128)} %all-gather.10.cloned.1.call-done) | copy-start | bytes 7864324
  1251.1 5.0 copy-start.1
  1258.0 3.3 copy-start.11
  1258.0 5.4 copy-start.2
  1259.6 5.2 copy-start.20
  1261.3 5.7 copy-start.7
  1264.1 0.7 copy-start.4
  1271.0 3.1 copy-start.8
  1271.0 3.9 copy-start.3
  1271.0 4.3 copy-start.5
  1274.4 2.2 copy-start.10
  1274.4 2.2 copy-start.16
  1274.4 2.2 copy-start.21
  1275.2 6.8 copy-start.14
  1276.2 3.5 copy-start.22
  1276.7 4.7 copy-start.17
  1279.7 3.9 copy-start.13
  1283.2 3.3 copy-start.18
  1283.2 3.3 copy-start.6
  1283.2 3.3 copy-start.12
  1283.6 3.0 copy-start.15
  1284.2 2.4 copy-start.9
Sparse Core Ops, SparseCore 0:
  136.7 114.1 all-reduce.6
  763.6 482.9 all-reduce.4
Sparse Core Ops, SparseCore 1:
  139.2 67.6 all-gather.7
  253.7 107.1 reduce-scatter.10
  363.8 105.2 reduce-scatter.8
  471.2 70.2 all-gather.9
  544.2 104.1 reduce-scatter.6
  651.4 105.3 reduce-scatter.4
  758.8 70.6 all-gather.11
where the time goes:
time: 1300 us; the launch traced here: 1290 us
  waiting for transfers between devices  1080 us (83%)
  blocking collectives  125 us (10%)
  matrix products  53.2 us (4%)
  between operations  16.7 us (1%)
    psum x1, waiting for transfers between devices, per_device(): summed = lax.psum(local_gram, ('prow', 'pcol'))  417 us
    reduce_scatter x4, waiting for transfers between devices, reduce_one(): lax.psum_scatter(term(jnp.int32(0), lax.axis_size('pcol') * count), 'pcol...  410 us
    all_gather x4, blocking collectives, rows_one(): return lax.all_gather(piece, 'pcol', axis=1, tiled=True)  125 us
    psum x1, waiting for transfers between devices, from_root(): return lax.psum(jnp.where(mine, array, jnp.zeros_like(array)), axis)  114 us
    all_gather x1, waiting for transfers between devices, per_device(): lax.all_gather(factor_top, 'pcol', axis=1, tiled=True)  72.4 us
    all_gather x1, waiting for transfers between devices, per_device(): lax.all_gather(adjoint_top, 'pcol', axis=1, tiled=True)  65.2 us
    dot_general x30, matrix products, matmul(): jnp.dot(left, right, precision=HIGHEST, preferred_element_type=jnp.float32)  27.1 us
  transfers between devices with their start and end apart: 9, of which 8 were waited for; matrix products, arithmetic and copies ran while one was open for 2% of the time, Pallas kernels for 0%

commit v1 on v0

--- a/solution.py
+++ b/solution.py
@@ -134,7 +134,7 @@
         local_gram = jnp.stack(
             [inner_product(lower_grads[panel], columns[:, earlier]) for earlier in range(panel + 1)]
         )
-        summed = lax.psum(local_gram, ("prow", "pcol"))
+        summed = lax.psum(lax.psum(local_gram, "pcol"), "prow")
         for earlier in range(panel + 1):
             grams[panel, earlier] = summed[earlier]
         top_step(panel)

time: 1300 us -> 1150 us (0.88)
  the two profiles are of different devices: /device:TPU:8 before, /device:TPU:1 now
where the time goes in v1:
time: 1150 us
  waiting for transfers between devices  934 us (81%)
  blocking collectives  126 us (11%)
  matrix products  53.2 us (5%)
  between operations  16.7 us (1%)
    reduce_scatter x4, waiting for transfers between devices, reduce_one(): lax.psum_scatter(term(jnp.int32(0), lax.axis_size('pcol') * count), 'pcol...  405 us
    psum x2, waiting for transfers between devices, per_device(): summed = lax.psum(lax.psum(local_gram, 'pcol'), 'prow')  264 us
    all_gather x4, blocking collectives, rows_one(): return lax.all_gather(piece, 'pcol', axis=1, tiled=True)  126 us
    psum x1, waiting for transfers between devices, from_root(): return lax.psum(jnp.where(mine, array, jnp.zeros_like(array)), axis)  112 us
    all_gather x1, waiting for transfers between devices, per_device(): lax.all_gather(factor_top, 'pcol', axis=1, tiled=True)  76.1 us
    all_gather x1, waiting for transfers between devices, per_device(): lax.all_gather(adjoint_top, 'pcol', axis=1, tiled=True)  74.6 us
    dot_general x30, matrix products, matmul(): jnp.dot(left, right, precision=HIGHEST, preferred_element_type=jnp.float32)  27.1 us
  transfers between devices with their start and end apart: 10, of which 9 were waited for; matrix products, arithmetic and copies ran while one was open for 2% of the time, Pallas kernels for 0%

profile of v1, /device:TPU:1, one launch (start us, length us, event | category | flops | bytes accessed | tf_op | source)
XLA Modules:
  0.0 1150.1 jit_solution(15074182320154749252)
XLA Ops:
  9.0 39.1 %all-gather.3 = f32[2,256,256]{2,1,0:T(8,128)S(1)} all-gather(f32[2,8,256]{2,1,0:T(8,128)S(1)} %get-tuple-element.19), channel_id=5, replica_groups=mesh['prow'=16,'pcol'=32] {'pcol'}, dimensions={1}, use_global_device_ids=true | all-gather | bytes 540672 | tf_op jit(solution)/shard_map/all_gather | solution.py:44
  48.1 28.5 %all-gather.2 = f32[2,256,256]{2,1,0:T(8,128)S(1)} all-gather(f32[2,8,256]{2,1,0:T(8,128)S(1)} %get-tuple-element.20), channel_id=4, replica_groups=mesh['prow'=16,'pcol'=32] {'pcol'}, dimensions={1}, use_global_device_ids=true | all-gather | bytes 540672 | tf_op jit(solution)/shard_map/all_gather | solution.py:44
  78.1 29.8 %all-gather.1 = f32[2,256,256]{2,1,0:T(8,128)S(1)} all-gather(f32[2,8,256]{2,1,0:T(8,128)S(1)} %get-tuple-element.21), channel_id=3, replica_groups=mesh['prow'=16,'pcol'=32] {'pcol'}, dimensions={1}, use_global_device_ids=true | all-gather | bytes 540672 | tf_op jit(solution)/shard_map/all_gather | solution.py:44
  108.6 28.5 %all-gather = f32[2,256,256]{2,1,0:T(8,128)S(1)} all-gather(f32[2,8,256]{2,1,0:T(8,128)S(1)} %get-tuple-element.18), channel_id=2, replica_groups=mesh['prow'=16,'pcol'=32] {'pcol'}, dimensions={1}, use_global_device_ids=true | all-gather | bytes 540672 | tf_op jit(solution)/shard_map/all_gather | solution.py:44
  138.5 112.3 %all-reduce.11.cloned.1.call-done = (f32[256,256]{1,0:T(8,128)}, f32[256,256]{1,0:T(8,128)}, f32[256,256]{1,0:T(8,128)}, f32[256,256]{1,0:T(8,128)}) async-done(((f32[256,256]{1,0:T(8,128)}, f32[256,256]{1,0:T(8,128)}, f32[256,256]{1,0:T(8,128)}, f32[256,256]{1,0:T(8,128)}), (f32[256,256]{1,0:T(8,128)}, f32[256,256]{1,0:T(8,128)}, f32[256,256]{1,0:T(8,128)}, ...) | async-done | bytes 1048592 | tf_op jit(solution)/shard_map/psum | solution.py:13
  250.8 1.7 convolution_bitcast_fusion
  252.5 1.1 copy.31
  254.4 1.1 copy.29
  257.0 1.1 copy.27
  259.0 1.1 copy.25
  260.2 98.6 %reduce-scatter.11.cloned.1.call-done = f32[16,256]{1,0:T(8,128)} async-done(((f32[512,256]{1,0:T(8,128)}), f32[16,256]{1,0:T(8,128)}) %reduce-scatter.11.cloned.1.call-update) | async-done | bytes 16400 | tf_op jit(solution)/shard_map/reduce_scatter | solution.py:52
  358.8 1.2 fusion.67
  361.7 1.0 pad_maximum_fusion
  362.7 104.0 %reduce-scatter.9.cloned.1.call-done = f32[16,256]{1,0:T(8,128)} async-done(((f32[512,256]{1,0:T(8,128)}), f32[16,256]{1,0:T(8,128)}) %reduce-scatter.9.cloned.1.call-update) | async-done | bytes 16400 | tf_op jit(solution)/shard_map/reduce_scatter | solution.py:52
  466.7 76.1 %all-gather.10.cloned.1.call-done = f32[10,256,256]{2,1,0:T(8,128)} async-done(((f32[10,8,256]{2,1,0:T(8,128)}), f32[10,256,256]{2,1,0:T(8,128)}) %all-gather.10.cloned.1.call-update) | async-done | bytes 2621456 | tf_op jit(solution)/shard_map/all_gather | solution.py:89
  542.7 1.3 convolution_subtract_fusion.19
  544.1 1.1 fusion.70
  546.5 100.2 %reduce-scatter.7.cloned.1.call-done = f32[16,256]{1,0:T(8,128)} async-done(((f32[512,256]{1,0:T(8,128)}), f32[16,256]{1,0:T(8,128)}) %reduce-scatter.7.cloned.1.call-update) | async-done | bytes 16400 | tf_op jit(solution)/shard_map/reduce_scatter | solution.py:52
  646.7 1.2 convolution_subtract_fusion.18
  647.9 1.2 convolution_subtract_fusion.17
  649.1 1.1 fusion.74
  650.2 1.1 convolution_bitcast_fusion.11
  651.4 1.1 convolution_bitcast_fusion.12
  652.5 102.3 %reduce-scatter.5.cloned.1.call-done = f32[16,256]{1,0:T(8,128)} async-done(((f32[512,256]{1,0:T(8,128)}), f32[16,256]{1,0:T(8,128)}) %reduce-scatter.5.cloned.1.call-update) | async-done | bytes 16400 | tf_op jit(solution)/shard_map/reduce_scatter | solution.py:52
  756.2 1.2 fusion.79
  757.4 1.1 convolution_bitcast_fusion.13
  758.6 1.9 pad_maximum_fusion.2
  762.3 216.0 %all-reduce.7.cloned.1.call-done = (f32[2,256,256]{2,1,0:T(8,128)}, f32[3,256,256]{2,1,0:T(8,128)}, f32[4,256,256]{2,1,0:T(8,128)}, f32[1,256,256]{2,1,0:T(8,128)}) async-done(((f32[2,256,256]{2,1,0:T(8,128)}, f32[3,256,256]{2,1,0:T(8,128)}, f32[4,256,256]{2,1,0:T(8,128)}, f32[1,256,256]{2,1,0:T(8,128)}), (f32[2,256,256]{2,1,0:T(8,128)}, f32[3,256,256]{2,1,0:T(8,128)}, f32[4,256,256]{2,1,0:T(8,128)}, ...) | async-done | bytes 2621456 | tf_op jit(solution)/shard_map/psum | solution.py:137
  979.1 74.6 %all-gather.12.cloned.1.call-done = f32[10,256,256]{2,1,0:T(8,128)} async-done(((f32[10,8,256]{2,1,0:T(8,128)}), f32[10,256,256]{2,1,0:T(8,128)}) %all-gather.12.cloned.1.call-update) | async-done | bytes 2621456 | tf_op jit(solution)/shard_map/all_gather | solution.py:90
  1053.6 48.2 %all-reduce.9.cloned.1.call-done = (f32[2,256,256]{2,1,0:T(8,128)}, f32[3,256,256]{2,1,0:T(8,128)}, f32[4,256,256]{2,1,0:T(8,128)}, f32[1,256,256]{2,1,0:T(8,128)}) async-done(((f32[2,256,256]{2,1,0:T(8,128)}, f32[3,256,256]{2,1,0:T(8,128)}, f32[4,256,256]{2,1,0:T(8,128)}, f32[1,256,256]{2,1,0:T(8,128)}), (f32[2,256,256]{2,1,0:T(8,128)}, f32[3,256,256]{2,1,0:T(8,128)}, f32[4,256,256]{2,1,0:T(8,128)}, ...) | async-done | bytes 2621456 | tf_op jit(solution)/shard_map/psum | solution.py:137
  1101.8 1.5 fusion.18
  1103.4 1.3 fusion.62
  1104.7 1.5 fusion.66
  1106.5 1.5 fusion.8
  1108.0 1.3 fusion.69
  1109.3 1.6 fusion.7
  1113.3 1.5 fusion.5
  1115.2 1.3 fusion.72
  1116.6 1.5 fusion.6
  1119.9 1.6 convolution_subtract_fusion.11
  1123.0 1.3 fusion.71
  1124.3 1.8 copy.38
  1126.1 1.5 fusion.1
  1127.6 1.5 fusion.2
  1132.0 1.4 fusion.3
  1135.1 1.6 convolution_subtract_fusion.6
  1139.8 1.0 bitcast_dynamic-update-slice_fusion.8
  1140.7 1.1 bitcast_dynamic-update-slice_fusion.7
  (141 shorter events, 28.5 us)
Async XLA Ops:
  8.0 242.8 %all-reduce.11.cloned.1.call-start = ((), (), s32[]{:S(2)}) async-start(), calls=%async_computation.13 | async-start | bytes 2097152 | tf_op jit(solution)/shard_map/psum | solution.py:13
  9.0 129.5 %copy-start.19 = (f32[2,1,256,1,1,256]{5,4,3,2,1,0:T(1,128)S(1)}, f32[2,1,256,1,1,256]{5,4,3,2,1,0:T(1,128)}, u32[]{:S(2)}) copy-start(f32[2,1,256,1,1,256]{5,4,3,2,1,0:T(1,128)} %param.6) | copy-start | bytes 1572868
  137.9 122.3 %all-gather.8.cloned.1.call-start = ((), (), s32[]{:S(2)}) async-start(), calls=%async_computation.8 | async-start | bytes 1081344 | tf_op jit(solution)/shard_map/all_gather | solution.py:91
  138.4 220.4 %reduce-scatter.11.cloned.1.call-start = ((), (), s32[]{:S(2)}) async-start(), calls=%async_computation.7 | async-start | bytes 540672 | tf_op jit(solution)/shard_map/reduce_scatter | solution.py:52
  250.8 2.8 copy-start.25
  250.8 5.5 copy-start.24
  253.6 213.1 %reduce-scatter.9.cloned.1.call-start = ((), (), s32[]{:S(2)}) async-start(), calls=%async_computation.6 | async-start | bytes 540672 | tf_op jit(solution)/shard_map/reduce_scatter | solution.py:52
  253.7 4.5 copy-start.27
  254.3 3.9 copy-start.26
  254.4 3.9 copy-start.23
  255.5 287.2 %all-gather.10.cloned.1.call-start = ((), (), s32[]{:S(2)}) async-start(), calls=%async_computation.9 | async-start | bytes 2703360 | tf_op jit(solution)/shard_map/all_gather | solution.py:89
  256.3 390.4 %reduce-scatter.7.cloned.1.call-start = ((), (), s32[]{:S(2)}) async-start(), calls=%async_computation.5 | async-start | bytes 540672 | tf_op jit(solution)/shard_map/reduce_scatter | solution.py:52
  258.1 496.7 %reduce-scatter.5.cloned.1.call-start = ((), (), s32[]{:S(2)}) async-start(), calls=%async_computation.4 | async-start | bytes 540672 | tf_op jit(solution)/shard_map/reduce_scatter | solution.py:52
  260.1 718.2 %all-reduce.7.cloned.1.call-start = ((), (), s32[]{:S(2)}) async-start(), calls=%async_computation.11 | async-start | bytes 5242880 | tf_op jit(solution)/shard_map/psum | solution.py:137
  542.7 212.1 %copy-start = (f32[10,256,256]{2,1,0:T(8,128)S(1)}, f32[10,256,256]{2,1,0:T(8,128)}, u32[]{:S(2)}) copy-start(f32[10,256,256]{2,1,0:T(8,128)} %all-gather.10.cloned.1.call-done) | copy-start | bytes 7864324
  761.4 292.2 %all-gather.12.cloned.1.call-start = ((), (), s32[]{:S(2)}) async-start(), calls=%async_computation.10 | async-start | bytes 2703360 | tf_op jit(solution)/shard_map/all_gather | solution.py:90
  762.0 339.8 %all-reduce.9.cloned.1.call-start = ((), (), s32[]{:S(2)}) async-start(), calls=%async_computation.12 | async-start | bytes 5242880 | tf_op jit(solution)/shard_map/psum | solution.py:137
  1106.4 5.0 copy-start.1
  1113.3 3.3 copy-start.11
  1113.3 5.4 copy-start.2
  1114.8 5.0 copy-start.20
  1116.6 5.5 copy-start.7
  1119.1 0.7 copy-start.4
  1126.1 3.1 copy-start.8
  1126.1 3.9 copy-start.3
  1126.1 4.3 copy-start.5
  1129.5 2.4 copy-start.10
  1129.6 2.4 copy-start.16
  1129.6 2.4 copy-start.21
  1130.4 7.0 copy-start.14
  1131.6 3.5 copy-start.22
  1132.0 4.7 copy-start.17
  1135.1 3.9 copy-start.13
  1138.5 3.3 copy-start.18
  1138.5 3.3 copy-start.6
  1138.5 3.3 copy-start.12
  1139.0 3.0 copy-start.15
  1139.6 2.4 copy-start.9
Sparse Core Ops, SparseCore 0:
  138.0 112.7 all-reduce.10
  978.4 123.4 all-reduce.8
Sparse Core Ops, SparseCore 1:
  140.5 67.5 all-gather.7
  253.7 105.0 reduce-scatter.10
  361.7 104.9 reduce-scatter.8
  468.8 73.8 all-gather.9
  545.5 101.1 reduce-scatter.6
  649.7 105.1 reduce-scatter.4
  761.5 216.7 all-reduce.6
  980.5 73.1 all-gather.11
